TPU v7x, 128 devices: a whole 4x4x4 slice. The times are simulated.
128 devices in a mesh: section: 8 (over z, core), space: 16 (over y, x).
Axes of the slice: x: 4, y: 4, z: 4, core: 2. Of those that a mesh axis runs over, the one named last changes fastest.
Arguments:
- inputs: bfloat16 [4, 64, 16, 2, 128], P(None, None, 'space'), may hold values from -6 to 6
- cotangent: bfloat16 [4, 64, 16, 2, 128], P(None, None, 'space'), may hold values from -6 to 6
- conv_weight: bfloat16 [2, 8, 128, 1728], P(None, 'section'), may hold values from -0.15625 to 0.15625
- mix_weight: bfloat16 [2, 8, 64, 128], P(None, 'section'), may hold values from -0.5 to 0.5
Outputs:
- conv_grad: float32 [2, 8, 128, 1728], P(None, 'section')
- mix_grad: float32 [2, 8, 64, 128], P(None, 'section')
All inputs are finite; a program needn't handle non-finite values.
Results may differ from a plain program's by a relative error of at most 0.03.
Values may be sent and summed in bfloat16 or wider, within the bound.
A program may use at most 64 MiB of HBM per device.

v0:
```python
import math

import jax
import jax.numpy as jnp
from jax import lax
from jax.sharding import PartitionSpec as P


def padded_2(block, sides, width):
    for axis, dim in sides:
        count = lax.axis_size(axis)
        forward = [(i, i + 1) for i in range(count - 1)]
        backward = [(target, source) for source, target in forward]
        low = lax.ppermute(
            lax.slice_in_dim(block, block.shape[dim] - width, None, axis=dim), axis, forward
        )
        high = lax.ppermute(lax.slice_in_dim(block, 0, width, axis=dim), axis, backward)
        block = jnp.concatenate([low, block, high], axis=dim)
    return block


def from_behind(block, axis, distance):
    devices = range(lax.axis_size(axis))
    route = [((i - distance) % len(devices), i) for i in devices]
    return lax.ppermute(block, axis, route)


def columns(padded, flip_sign, extent_x, extent_y, extent_z):
    pieces = []
    for step_x in (-1, 0, 1):
        for step_y in (-1, 0, 1):
            for step_z in (-1, 0, 1):
                start_x = 1 + flip_sign * step_x
                start_y = 1 + flip_sign * step_y
                start_z = 1 + flip_sign * step_z
                pieces.append(
                    padded[
                        :,
                        start_x : start_x + extent_x,
                        start_y : start_y + extent_y,
                        start_z : start_z + extent_z,
                    ]
                )
    stacked = jnp.stack(pieces, 0)
    return stacked.reshape(27 * padded.shape[0], extent_x * extent_y * extent_z)


def silu_slope(preact):
    sigmoid_val = jax.nn.sigmoid(preact)
    return sigmoid_val * (1.0 + preact * (1.0 - sigmoid_val))


def transpose_conv(conv_w, channels):
    hidden_count = conv_w.shape[0]
    return (
        conv_w.reshape(hidden_count, 27, channels)
        .transpose(2, 1, 0)
        .reshape(channels, 27 * hidden_count)
    )


def pad_sides(rimmed):
    return jnp.pad(rimmed, ((0, 0), (0, 0), (1, 1), (1, 1)))


def pick_pair(store, first_index, second_index):
    zero_index = jnp.zeros((), jnp.int32)
    starts = (first_index, second_index) + (zero_index,) * (store.ndim - 2)
    return lax.dynamic_slice(store, starts, (1, 1) + store.shape[2:])[0, 0]


def place_pair(store, value, first_index, second_index, active):
    zero_index = jnp.zeros((), jnp.int32)
    starts = (first_index, second_index) + (zero_index,) * (store.ndim - 2)
    current = pick_pair(store, first_index, second_index)
    chosen = jnp.where(active, value, current)
    return lax.dynamic_update_slice(store, chosen[None, None], starts)


def place_one(store, value, index_value, active):
    current = lax.dynamic_index_in_dim(store, index_value, 0, keepdims=False)
    chosen = jnp.where(active, value, current)
    return lax.dynamic_update_index_in_dim(store, chosen, index_value, 0)


def per_device(inputs, cotangent, conv_weight, mix_weight):
    micro_count, channels, extent_x, extent_y, extent_z = inputs.shape
    layer_groups = conv_weight.shape[0]
    hidden_count = conv_weight.shape[2]
    section_count = lax.axis_size("section")
    section_index = lax.axis_index("section")
    layer_count = layer_groups * section_count
    cell_count = extent_x * extent_y * extent_z
    conv_local = conv_weight[:, 0]
    mix_local = mix_weight[:, 0]
    flipped_local = jnp.stack(
        [transpose_conv(conv_local[layer_group], channels) for layer_group in range(layer_groups)],
        0,
    )
    delay_ticks = micro_count - 1
    tick_total = micro_count + layer_count - 1 + (layer_groups - 1) * delay_ticks
    tick_values = jnp.arange(tick_total, dtype=jnp.int32)

    def locate(tick_index, position):
        group_index = jnp.zeros((), jnp.int32)
        micro_index = jnp.zeros((), jnp.int32)
        active = tick_index < 0
        for layer_group in range(layer_groups):
            offset = tick_index - layer_group * (section_count + delay_ticks) - position
            inside = (offset >= 0) & (offset < micro_count)
            group_index = jnp.where(inside, jnp.int32(layer_group), group_index)
            micro_index = jnp.where(inside, offset, micro_index)
            active = active | inside
        return (group_index, micro_index, active)

    def store_returned(returned, incoming, tick_index):
        back_index = tick_index - section_count
        back_valid = (back_index >= 0) & (back_index < micro_count)
        back_safe = jnp.clip(back_index, 0, micro_count - 1)
        return place_one(returned, incoming, back_safe, back_valid)

    def forward_layer(activation, conv_w, mix_w):
        act_low = activation.astype(jnp.bfloat16)
        rimmed = padded_2(act_low, (("space", 1),), 1)
        window = columns(pad_sides(rimmed), 1, extent_x, extent_y, extent_z)
        preact = jnp.dot(conv_w, window, preferred_element_type=jnp.float32)
        hidden = jax.nn.silu(preact).astype(jnp.bfloat16)
        mixed_term = jnp.dot(mix_w, hidden, preferred_element_type=jnp.float32)
        result = activation.reshape(channels, cell_count) + mixed_term
        return (result.reshape(activation.shape), rimmed, preact, act_low)

    field_shape = (channels, extent_x, extent_y, extent_z)
    stores = jnp.zeros((layer_groups, micro_count) + field_shape, jnp.bfloat16)

    def forward_tick(carry, tick_index):
        incoming, returned, kept = carry
        layer_group, micro_index, active = locate(tick_index, section_index)
        returned = store_returned(returned, incoming, tick_index)
        fresh = lax.dynamic_index_in_dim(inputs, micro_index, 0, keepdims=False).astype(jnp.float32)
        looped = lax.dynamic_index_in_dim(returned, micro_index, 0, keepdims=False)
        first_section = jnp.where(layer_group == 0, fresh, looped)
        source = jnp.where(section_index == 0, first_section, incoming)
        conv_w = lax.dynamic_index_in_dim(conv_local, layer_group, 0, keepdims=False)
        mix_w = lax.dynamic_index_in_dim(mix_local, layer_group, 0, keepdims=False)
        result, rimmed, preact, act_low = forward_layer(source, conv_w, mix_w)
        kept = place_pair(kept, act_low, layer_group, micro_index, active)
        outgoing = from_behind(result, "section", 1)
        return ((outgoing, returned, kept), None)

    empty_field = jnp.zeros(field_shape, jnp.float32)
    empty_returned = jnp.zeros((micro_count,) + field_shape, jnp.float32)
    forward_state, unused = lax.scan(
        forward_tick, (empty_field, empty_returned, stores), tick_values
    )
    stores = forward_state[2]
    position = section_count - 1 - section_index

    def backward_tick(carry, tick_index):
        incoming, returned, conv_sum, mix_sum = carry
        mirror_group, micro_index, active = locate(tick_index, position)
        layer_group = layer_groups - 1 - mirror_group
        returned = store_returned(returned, incoming, tick_index)
        seed_grad = lax.dynamic_index_in_dim(cotangent, micro_index, 0, keepdims=False).astype(
            jnp.float32
        )
        looped = lax.dynamic_index_in_dim(returned, micro_index, 0, keepdims=False)
        last_section = jnp.where(mirror_group == 0, seed_grad, looped)
        upstream = jnp.where(position == 0, last_section, incoming)
        conv_w = lax.dynamic_index_in_dim(conv_local, layer_group, 0, keepdims=False)
        mix_w = lax.dynamic_index_in_dim(mix_local, layer_group, 0, keepdims=False)
        flipped = lax.dynamic_index_in_dim(flipped_local, layer_group, 0, keepdims=False)
        activation = pick_pair(stores, layer_group, micro_index)
        rimmed = padded_2(activation, (("space", 1),), 1)
        window = columns(pad_sides(rimmed), 1, extent_x, extent_y, extent_z)
        preact = jnp.dot(conv_w, window, preferred_element_type=jnp.float32)
        hidden = jax.nn.silu(preact).astype(jnp.bfloat16)
        flat_up = upstream.reshape(channels, cell_count)
        up_low = flat_up.astype(jnp.bfloat16)
        mix_term = jnp.dot(up_low, hidden.T, preferred_element_type=jnp.float32)
        hid_grad = jnp.dot(mix_w.T, up_low, preferred_element_type=jnp.float32)
        pre_grad = (hid_grad * silu_slope(preact)).astype(jnp.bfloat16)
        conv_term = jnp.dot(pre_grad, window.T, preferred_element_type=jnp.float32)
        grad_field = pre_grad.reshape(hidden_count, extent_x, extent_y, extent_z)
        grad_rimmed = padded_2(grad_field, (("space", 1),), 1)
        back_window = columns(pad_sides(grad_rimmed), -1, extent_x, extent_y, extent_z)
        spread = jnp.dot(flipped, back_window, preferred_element_type=jnp.float32)
        downstream = (flat_up + spread).reshape(field_shape)
        conv_now = lax.dynamic_index_in_dim(conv_sum, layer_group, 0, keepdims=False)
        mix_now = lax.dynamic_index_in_dim(mix_sum, layer_group, 0, keepdims=False)
        conv_sum = lax.dynamic_update_index_in_dim(
            conv_sum, jnp.where(active, conv_now + conv_term, conv_now), layer_group, 0
        )
        mix_sum = lax.dynamic_update_index_in_dim(
            mix_sum, jnp.where(active, mix_now + mix_term, mix_now), layer_group, 0
        )
        outgoing = from_behind(downstream, "section", -1)
        return ((outgoing, returned, conv_sum, mix_sum), None)

    conv_start = jnp.zeros((layer_groups, hidden_count, 27 * channels), jnp.float32)
    mix_start = jnp.zeros((layer_groups, channels, hidden_count), jnp.float32)
    backward_state, unused_back = lax.scan(
        backward_tick, (empty_field, empty_returned, conv_start, mix_start), tick_values
    )
    conv_total, mix_total = lax.psum((backward_state[2], backward_state[3]), "space")
    factor = 1.0 / math.sqrt(micro_count * extent_x * lax.axis_size("space") * extent_y * extent_z)
    return ((conv_total * factor)[:, None], (mix_total * factor)[:, None])


def solution(mesh):
    placed = (
        P(None, None, "space", None, None),
        P(None, None, "space", None, None),
        P(None, "section", None, None),
        P(None, "section", None, None),
    )
    return jax.shard_map(
        per_device,
        mesh=mesh,
        in_specs=placed,
        out_specs=(P(None, "section", None, None), P(None, "section", None, None)),
        check_vma=False,
    )
```

profile of v0, /device:TPU:32, one launch (start us, length us, event | category | flops | bytes accessed | tf_op | source)
XLA Modules:
  0.0 1613.7 jit_solution(14105221133534441450)
XLA Ops:
  11.5 488.7 %while.34 = (s32[]{:T(128)}, f32[64,1,2,128]{3,2,0,1:T(2,128)S(1)}, f32[4,64,1,2,128]{4,3,1,2,0:T(2,128)S(1)}, bf16[2,4,64,1,2,128]{5,4,2,3,1,0:T(2,128)(2,1)S(1...) while((s32[]{:T(128)}, f32[64,1,2,128]{3,2,0,1:T(2,128)S(1)}, ...), condition=%wide.region_1.2_spmd, body=%wide.region_0.1_spmd.sunk | while | flops 119616024 | bytes 4936221 | solution.py:152
  57.2 4.7 collective-permute-start.1
  178.8 4.9 collective-permute-done.2
  201.5 4.9 collective-permute-done.2
  224.1 4.9 collective-permute-done.2
  246.7 4.9 collective-permute-done.2
  269.3 4.9 collective-permute-done.2
  291.9 4.9 collective-permute-done.2
  314.5 4.9 collective-permute-done.2
  337.1 4.9 collective-permute-done.2
  359.7 4.9 collective-permute-done.2
  382.3 4.9 collective-permute-done.2
  404.9 4.9 collective-permute-done.2
  427.5 4.9 collective-permute-done.2
  450.1 4.9 collective-permute-done.2
  472.7 4.9 collective-permute-done.2
  495.3 4.9 collective-permute-done.2
  501.3 1002.2 %while.35 = (s32[]{:T(128)}, f32[64,1,2,128]{3,2,0,1:T(2,128)S(1)}, f32[4,64,1,2,128]{4,3,1,2,0:T(2,128)S(1)}, f32[2,128,1728]{1,2,0:T(8,128)S(1)}, f32[2,64,128...) while((s32[]{:T(128)}, f32[64,1,2,128]{3,2,0,1:T(2,128)S(1)}, ...), condition=%wide.region_3.4_spmd, body=%wide.region_2.3_spmd.sunk | while | flops 354833920 | bytes 30681180 | solution.py:201
  503.7 4.6 collective-permute-start.4
  523.8 4.3 collective-permute-start.6
  568.2 6.2 collective-permute-start.6
  595.7 4.2 collective-permute-start.4
  615.4 6.2 collective-permute-start.6
  640.3 4.5 collective-permute-start.4
  660.2 5.9 collective-permute-start.6
  705.3 6.2 collective-permute-start.6
  731.2 4.2 collective-permute-start.4
  750.9 6.2 collective-permute-start.6
  776.7 4.2 collective-permute-start.4
  796.4 6.2 collective-permute-start.6
  842.0 6.2 collective-permute-start.6
  867.9 4.2 collective-permute-start.4
  887.6 6.2 collective-permute-start.6
  913.4 4.2 collective-permute-start.4
  933.1 6.2 collective-permute-start.6
  978.7 6.2 collective-permute-start.6
  1024.2 6.2 collective-permute-start.6
  1069.8 6.2 collective-permute-start.6
  1115.3 6.2 collective-permute-start.6
  1160.9 6.2 collective-permute-start.6
  1206.5 6.2 collective-permute-start.6
  1252.0 6.2 collective-permute-start.6
  1297.6 6.2 collective-permute-start.6
  1343.1 6.2 collective-permute-start.6
  1388.7 6.2 collective-permute-start.6
  1434.2 6.2 collective-permute-start.6
  1479.8 6.2 collective-permute-start.6
  1504.8 98.7 %all-reduce.6.cloned.1.call-done = (f32[2,128,1728]{1,2,0:T(8,128)}, f32[2,64,128]{2,1,0:T(8,128)}) async-done(((f32[2,128,1728]{1,2,0:T(8,128)}, f32[2,64,128]{2,1,0:T(8,128)}), (f32[2,128,1728]{1,2,0:T(8,128)}, f32[2,64,128]{2,1,0:T(8,128)})) %all-reduce.6.cloned.1.call-update) | async-done | bytes 1835024 | tf_op jit(solution)/shard_map/psum | solution.py:204
  (3287 shorter events, 1133.5 us)
Async XLA Ops:
  7.2 1596.3 %all-reduce.6.cloned.1.call-start = ((), (), s32[]{:S(2)}) async-start(), calls=%async_computation | async-start | bytes 3670016 | tf_op jit(solution)/shard_map/psum | solution.py:204
  503.7 9.6 collective-permute-start.4
  523.8 7.7 collective-permute-start.6
  528.1 6.5 collective-permute-start.5
  549.0 8.7 collective-permute-start.4
  568.2 9.6 collective-permute-start.6
  574.3 6.5 collective-permute-start.5
  595.7 9.2 collective-permute-start.4
  615.4 9.6 collective-permute-start.6
  621.6 6.5 collective-permute-start.5
  640.3 9.5 collective-permute-start.4
  660.2 9.3 collective-permute-start.6
  685.6 9.2 collective-permute-start.4
  705.3 9.6 collective-permute-start.6
  731.2 9.2 collective-permute-start.4
  750.9 9.6 collective-permute-start.6
  776.7 9.2 collective-permute-start.4
  796.4 9.6 collective-permute-start.6
  822.3 9.2 collective-permute-start.4
  842.0 9.6 collective-permute-start.6
  867.9 9.2 collective-permute-start.4
  887.6 9.6 collective-permute-start.6
  913.4 9.2 collective-permute-start.4
  933.1 9.6 collective-permute-start.6
  959.0 9.2 collective-permute-start.4
  978.7 9.6 collective-permute-start.6
  1004.5 9.2 collective-permute-start.4
  1024.2 9.6 collective-permute-start.6
  1050.1 9.2 collective-permute-start.4
  1069.8 9.6 collective-permute-start.6
  1095.6 9.2 collective-permute-start.4
  1115.3 9.6 collective-permute-start.6
  1141.2 9.2 collective-permute-start.4
  1160.9 9.6 collective-permute-start.6
  1186.8 9.2 collective-permute-start.4
  1206.5 9.6 collective-permute-start.6
  1232.3 9.2 collective-permute-start.4
  1252.0 9.6 collective-permute-start.6
  1277.9 9.2 collective-permute-start.4
  1297.6 9.6 collective-permute-start.6
  1323.4 9.2 collective-permute-start.4
  1343.1 9.6 collective-permute-start.6
  1369.0 9.2 collective-permute-start.4
  1388.7 9.6 collective-permute-start.6
  1414.5 9.2 collective-permute-start.4
  1434.2 9.6 collective-permute-start.6
  1460.1 9.2 collective-permute-start.4
  1479.8 9.6 collective-permute-start.6
  (443 other events, 2283.7 us)
Sparse Core Ops, SparseCore 0:
  1504.9 98.5 all-reduce.5
where the time goes:
time: 1630 us; the launch traced here: 1610 us
  starting transfers between devices  423 us (26%)
  waiting for transfers between devices  423 us (26%)
  local copies, waits for them, and re-layouts  410 us (25%)
  other arithmetic  142 us (9%)
  loops' own time  126 us (8%)
  matrix products  75.3 us (5%)
    ppermute x66, starting transfers between devices, padded_2(): lax.ppermute(lax.slice_in_dim(block, block.shape[dim] - width, None, axis...  315 us
    while x2332, local copies, waits for them, and re-layouts  297 us
    ppermute x66, waiting for transfers between devices, padded_2(): lax.ppermute(lax.slice_in_dim(block, 0, width, axis=dim), axis, backward)  180 us
    ppermute x44, waiting for transfers between devices, from_behind(): return lax.ppermute(block, axis, route)  138 us
    psum x1, waiting for transfers between devices, per_device(): lax.psum((backward_state[2], backward_state[3]), 'space')  98.7 us
    ppermute x66, starting transfers between devices, padded_2(): lax.ppermute(lax.slice_in_dim(block, 0, width, axis=dim), axis, backward)  84.7 us
    concatenate x66, other arithmetic, padded_2(): block = jnp.concatenate([low, block, high], axis=dim)  83.6 us
    another operation x1, loops' own time, per_device(): lax.scan(backward_tick, (empty_field, empty_returned, conv_start, mix_sta...  68.2 us
  transfers between devices with their start and end apart: 177, of which 133 were waited for; matrix products, arithmetic and copies ran while one was open for 6% of the time, Pallas kernels for 0%

commit v1 on v0

v1 whole, which is shorter than its diff:
```python
import functools
import math

import jax
import jax.numpy as jnp
from jax import lax
from jax.experimental import pallas as pl
from jax.experimental.pallas import tpu as pltpu
from jax.sharding import PartitionSpec as P

NZ = 128
PLANES = 8
BLOCKS = 16
KC = 128
HC = 256
F32 = jnp.float32
BF16 = jnp.bfloat16
MESH = pl.DeviceIdType.MESH
NT = (((1,), (1,)), ((), ()))
TN = (((0,), (0,)), ((), ()))
FWD_CHUNKS = ((1, 2), (3, 2), (5, 3))
BWD_CHUNKS = ((1, 2), (3, 2), (5, 3))


def rows_of(start, count):
    return pl.ds(pl.multiple_of(start * NZ, NZ), count * NZ)


def shifted(value, step):
    planes = value.shape[0] // NZ
    rolled = pltpu.roll(value, (-step) % value.shape[0], 0)
    row = lax.broadcasted_iota(jnp.int32, value.shape, 0) % NZ
    edge = NZ - 1 if step == 1 else 0
    return jnp.where(row == edge, 0.0, rolled)


def widen(value):
    return jnp.concatenate(
        [shifted(value, -1).astype(BF16), value.astype(BF16), shifted(value, 1).astype(BF16)], axis=1
    )


def chain_kernel(
    block_shift,
    x_ref, cot_ref, w_ref, mf_ref, mb_ref,
    g_ref, gm_ref,
    a3a, a3b, act, slope, sa3, shid, pga, pgb,
    fsend, frecv, bsend, brecv,
):
    section = lax.axis_index("section")
    core = lax.rem(section, 2)
    partner = section + 1 - 2 * core
    mine = lax.axis_index("space") + block_shift
    sign = 2 * core - 1

    def globally(local):
        return 7 + core + sign * local

    zeros3 = jnp.zeros((NZ, 3 * KC), BF16)
    for a3 in (a3a, a3b):
        a3[9 * NZ : 10 * NZ, :] = zeros3
    for pg in (pga, pgb):
        pg[9 * NZ : 10 * NZ, :] = jnp.zeros((NZ, HC), BF16)
    for local in range(-1, PLANES):
        tile = x_ref[globally(local)].astype(F32)
        if local >= 0:
            act[local * NZ : (local + 1) * NZ, :] = tile
        a3a[(local + 1) * NZ : (local + 2) * NZ, :] = widen(tile)

    def forward_planes(cur, nxt, block, first, count):
        rows = slice(first * NZ, (first + count) * NZ)
        window = jnp.concatenate(
            [
                cur[rows_of(first + 1 - sign, count), :],
                cur[(first + 1) * NZ : (first + 1 + count) * NZ, :],
                cur[rows_of(first + 1 + sign, count), :],
            ],
            axis=1,
        )
        pre = jnp.dot(window, w_ref[block], preferred_element_type=F32)
        sg = 0.5 + 0.5 * jnp.tanh(0.5 * pre)
        hid = pre * sg
        slope[block, rows, :] = (sg + hid * (1.0 - sg)).astype(BF16)
        hid = hid.astype(BF16)

        @pl.when(block == mine)
        def _():
            shid[rows, :] = hid

        new = act[rows, :] + jnp.dot(hid, mf_ref[block], preferred_element_type=F32)
        act[rows, :] = new
        nxt[(first + 1) * NZ : (first + 1 + count) * NZ, :] = widen(new)

    def act_copy(buf, par):
        return pltpu.make_async_remote_copy(
            src_ref=buf.at[pl.ds(NZ, NZ)],
            dst_ref=buf.at[pl.ds(0, NZ)],
            send_sem=fsend.at[par],
            recv_sem=frecv.at[par],
            device_id={"section": partner},
            device_id_type=MESH,
        )

    def forward_block(block, cur, nxt, par, wait, send):
        for first, count in FWD_CHUNKS:
            forward_planes(cur, nxt, block, first, count)
        wait(lambda: act_copy(cur, par).wait())

        @pl.when(block == mine)
        def _():
            sa3[...] = cur[...]

        forward_planes(cur, nxt, block, 0, 1)
        send(lambda: act_copy(nxt, 1 - par).start())

    def always(go):
        go()

    def forward_pair(step, carry):
        forward_block(2 * step, a3a, a3b, 0, lambda go: pl.when(step > 0)(go), always)
        forward_block(2 * step + 1, a3b, a3a, 1, always, lambda go: pl.when(step < 7)(go))
        return carry

    lax.fori_loop(0, BLOCKS // 2, forward_pair, 0)

    for local in range(PLANES):
        act[local * NZ : (local + 1) * NZ, :] = cot_ref[globally(local)].astype(F32)

    def backward_prep(pg, block, first, count):
        rows = slice(first * NZ, (first + count) * NZ)
        grad = jnp.dot(act[rows, :].astype(BF16), mb_ref[block], preferred_element_type=F32)
        pg[(first + 1) * NZ : (first + 1 + count) * NZ, :] = (
            grad * slope[block, rows, :].astype(F32)
        ).astype(BF16)

    def backward_planes(pg, block, first, count):
        rows = slice(first * NZ, (first + count) * NZ)
        spread = (
            lax.dot_general(
                pg[rows_of(first + 1 + sign, count), :], w_ref[block, 0:384], NT,
                preferred_element_type=F32,
            )
            + lax.dot_general(
                pg[(first + 1) * NZ : (first + 1 + count) * NZ, :], w_ref[block, 384:768], NT,
                preferred_element_type=F32,
            )
            + lax.dot_general(
                pg[rows_of(first + 1 - sign, count), :], w_ref[block, 768:1152], NT,
                preferred_element_type=F32,
            )
        )
        act[rows, :] = act[rows, :] + (
            shifted(spread[:, 0:128], 1) + spread[:, 128:256] + shifted(spread[:, 256:384], -1)
        )

    def grad_copy(buf, par):
        return pltpu.make_async_remote_copy(
            src_ref=buf.at[pl.ds(NZ, NZ)],
            dst_ref=buf.at[pl.ds(0, NZ)],
            send_sem=bsend.at[par],
            recv_sem=brecv.at[par],
            device_id={"section": partner},
            device_id_type=MESH,
        )

    def backward_block(block, pg, par, last):
        backward_prep(pg, block, 0, 1)
        last(lambda: grad_copy(pg, par).start())
        for first, count in BWD_CHUNKS:
            backward_prep(pg, block, first, count)

        @pl.when(block == mine)
        def _():
            own = pg[NZ : 9 * NZ, :]
            for dx in range(3):
                g_ref[:, dx * 384 : (dx + 1) * 384] = lax.dot_general(
                    own, sa3[rows_of(1 + (dx - 1) * sign, PLANES), :], TN,
                    preferred_element_type=F32,
                )
            gm_ref[...] = lax.dot_general(
                act[...].astype(BF16), shid[...], TN, preferred_element_type=F32
            )

        def rest():
            for first, count in BWD_CHUNKS:
                backward_planes(pg, block, first, count)
            grad_copy(pg, par).wait()
            backward_planes(pg, block, 0, 1)

        last(rest)

    def backward_pair(step, carry):
        backward_block(15 - 2 * step, pga, 0, always)
        backward_block(14 - 2 * step, pgb, 1, lambda go: pl.when(step < 7)(go))
        return carry

    lax.fori_loop(0, BLOCKS // 2, backward_pair, 0)


def run_chain(x, cot, w, mf, mb, block_shift=0):
    vmem = pl.BlockSpec(memory_space=pltpu.VMEM)
    return pl.pallas_call(
        functools.partial(chain_kernel, block_shift),
        out_shape=(
            jax.ShapeDtypeStruct((HC, 9 * KC), F32),
            jax.ShapeDtypeStruct((KC, HC), F32),
        ),
        in_specs=[vmem] * 5,
        out_specs=(vmem, vmem),
        scratch_shapes=[
            pltpu.VMEM((10 * NZ, 3 * KC), BF16),
            pltpu.VMEM((10 * NZ, 3 * KC), BF16),
            pltpu.VMEM((PLANES * NZ, KC), F32),
            pltpu.VMEM((BLOCKS, PLANES * NZ, HC), BF16),
            pltpu.VMEM((10 * NZ, 3 * KC), BF16),
            pltpu.VMEM((PLANES * NZ, HC), BF16),
            pltpu.VMEM((10 * NZ, HC), BF16),
            pltpu.VMEM((10 * NZ, HC), BF16),
            pltpu.SemaphoreType.DMA((2,)),
            pltpu.SemaphoreType.DMA((2,)),
            pltpu.SemaphoreType.DMA((2,)),
            pltpu.SemaphoreType.DMA((2,)),
        ],
        compiler_params=pltpu.CompilerParams(
            has_side_effects=True, vmem_limit_bytes=60 * 1024 * 1024
        ),
        name="chain",
    )(x, cot, w, mf, mb)


def conv_matrix(conv_w):
    taps = conv_w.reshape(-1, 128, 3, 3, 3, 64).transpose(0, 2, 3, 4, 5, 1)
    low, mid, high = taps[:, :, 0], taps[:, :, 1], taps[:, :, 2]
    top = jnp.concatenate([mid, low], axis=-1)
    bottom = jnp.concatenate([high, mid], axis=-1)
    return jnp.stack([top, bottom], axis=3).reshape(-1, 9 * KC, HC)


def mix_matrix(mix_w):
    empty = jnp.zeros_like(mix_w)
    return jnp.concatenate(
        [jnp.concatenate([mix_w, empty], 2), jnp.concatenate([empty, mix_w], 2)], 1
    )


def fold_conv(grad):
    parts = grad.reshape(2, 128, 3, 3, 2, 64)
    mid = parts[0, :, :, :, 0] + parts[1, :, :, :, 1]
    low = parts[1, :, :, :, 0]
    high = parts[0, :, :, :, 1]
    return jnp.stack([low, mid, high], axis=2).reshape(128, 1728)


def fold_mix(grad):
    return grad[0:64, 0:128] + grad[64:128, 128:256]


def plane_rows(tile):
    return tile[:, 0].transpose(2, 1, 0).reshape(NZ, KC)


def per_device(inputs, cotangent, conv_weight, mix_weight):
    section = lax.axis_index("section")
    space = lax.axis_index("space")
    micro = section // 2
    x = plane_rows(lax.dynamic_index_in_dim(inputs, micro, 0, keepdims=False))
    cot = plane_rows(lax.dynamic_index_in_dim(cotangent, micro, 0, keepdims=False))
    both = lax.all_gather(jnp.stack([x, cot], 0), "space")
    w = lax.all_gather(conv_matrix(conv_weight[:, 0]), "section")
    w = w.transpose(1, 0, 2, 3).reshape(BLOCKS, 9 * KC, HC)
    mix = lax.all_gather(mix_weight[:, 0], "section").transpose(1, 0, 2, 3).reshape(BLOCKS, 64, 128)
    mb = mix_matrix(mix)
    mf = mb.transpose(0, 2, 1)
    grad, grad_mix = run_chain(both[:, 0], both[:, 1], w, mf, mb)
    factor = 1.0 / math.sqrt(16384.0)
    part = jnp.concatenate([fold_conv(grad).reshape(-1, 128), fold_mix(grad_mix)], 0) * factor
    part = lax.psum(part, "section")
    slot = jnp.stack(
        [jnp.where(space == section, part, 0.0), jnp.where(space == section + 8, part, 0.0)], 0
    )
    total = lax.psum(slot, "space")
    return (
        total[:, :1728].reshape(2, 1, 128, 1728),
        total[:, 1728:].reshape(2, 1, 64, 128),
    )


def solution(mesh):
    placed = (
        P(None, None, "space", None, None),
        P(None, None, "space", None, None),
        P(None, "section", None, None),
        P(None, "section", None, None),
    )
    return jax.shard_map(
        per_device,
        mesh=mesh,
        in_specs=placed,
        out_specs=(P(None, "section", None, None), P(None, "section", None, None)),
        check_vma=False,
    )
```

time: 1630 us -> 370 us (0.23)
  starting transfers between devices: 423 us -> 0.16 us
  local copies, waits for them, and re-layouts: 410 us -> 21.1 us
  waiting for transfers between devices: 423 us -> 233 us
  other arithmetic: 142 us -> 5.25 us
  loops' own time: 126 us -> 0 us
  Pallas kernels: 0 us -> 82 us
  matrix products: 75.3 us -> 0 us
    ppermute x176 -> x0, starting transfers between devices: 423 us -> none  [the longest x66 315 us: padded_2(): lax.ppermute(lax.slice_in_dim(block, block.shape[dim] - width, None, axis...]
    ppermute x176 -> x0, waiting for transfers between devices: 324 us -> none  [the longest x66 180 us: padded_2(): lax.ppermute(lax.slice_in_dim(block, 0, width, axis=dim), axis, backward)]
    while x2332 -> x0, local copies, waits for them, and re-layouts: 297 us -> none
    another operation x2 -> x0, loops' own time: 126 us -> none  [the longest x1 68.2 us: per_device(): lax.scan(backward_tick, (empty_field, empty_returned, conv_start, mix_sta...]
    concatenate x66 -> x1, other arithmetic: 83.6 us -> 1.24 us  [mix_matrix(): jnp.concatenate([jnp.concatenate([mix_w, empty], 2), jnp.concatenate([emp...]
    pallas_call x0 -> x1, Pallas kernels: none -> 82 us  [run_chain(): pl.pallas_call(functools.partial(chain_kernel, block_shift), out_shape=(j...]
    all_gather x0 -> x2, waiting for transfers between devices: none -> 80 us  [the longest x1 52.7 us: per_device(): w = lax.all_gather(conv_matrix(conv_weight[:, 0]), 'section')]
    dot_general x132 -> x0, matrix products: 75.3 us -> none  [the longest x22 27.1 us: backward_tick(): conv_term = jnp.dot(pre_grad, window.T, preferred_element_type=jnp.float32)]
  transfers between devices with their start and end apart: 177 -> 4, of which waited for: 133 -> 4; matrix products, arithmetic and copies ran while one was open for 6% -> 2% of each run, Pallas kernels for 0% -> 0%
where the time goes in v1:
time: 370 us; the launch traced here: 369 us
  waiting for transfers between devices  233 us (63%)
  Pallas kernels  82 us (22%)
  local copies, waits for them, and re-layouts  21.1 us (6%)
  between operations  14 us (4%)
  blocking collectives  13.7 us (4%)
  other arithmetic  5.25 us (1%)
    psum x1, waiting for transfers between devices, per_device(): total = lax.psum(slot, 'space')  91.6 us
    pallas_call x1, Pallas kernels, run_chain(): pl.pallas_call(functools.partial(chain_kernel, block_shift), out_shape=(j...  82 us
    psum x1, waiting for transfers between devices, per_device(): part = lax.psum(part, 'section')  61.6 us
    all_gather x1, waiting for transfers between devices, per_device(): w = lax.all_gather(conv_matrix(conv_weight[:, 0]), 'section')  52.7 us
    all_gather x1, waiting for transfers between devices, per_device(): both = lax.all_gather(jnp.stack([x, cot], 0), 'space')  27.4 us
    all_gather x1, blocking collectives, per_device(): lax.all_gather(mix_weight[:, 0], 'section').transpose(1, 0, 2, 3)  13.7 us
  transfers between devices with their start and end apart: 4, of which 4 were waited for; matrix products, arithmetic and copies ran while one was open for 2% of the time, Pallas kernels for 0%

profile of v1, /device:TPU:32, one launch (start us, length us, event | category | flops | bytes accessed | tf_op | source)
XLA Modules:
  0.0 369.4 jit_solution(3215496985986207107)
XLA Ops:
  7.2 0.0 all-gather.7.cloned.1.call-start
  7.2 0.8 constant_dynamic-slice_fusion
  8.1 0.7 copy.34
  8.8 0.0 all-gather.7.cloned.1.call-update
  8.9 0.0 all-gather.5.cloned.1.call-start
  8.9 1.2 slice_bitcast_fusion.3
  10.1 0.1 maximum_bitcast_fusion
  10.3 0.1 pad_maximum_fusion.1
  10.4 0.0 copy-start
  10.4 1.1 copy.39
  11.5 0.0 all-gather.5.cloned.1.call-update
  11.6 0.0 all-reduce.5.cloned.1.call-start
  11.6 0.0 copy-done
  11.6 13.7 %all-gather.1 = bf16[16,1,64,128]{3,2,1,0:T(8,128)(2,1)S(1)} all-gather(bf16[2,1,64,128]{3,2,1,0:T(8,128)(2,1)S(1)} %copy-done), channel_id=3, replica_groups=mesh['section'=8,'space'=16] {'section'}, dimensions={0}, use_global_device_ids=true | all-gather | bytes 294912 | tf_op jit(solution)/shard_map/all_gather | solution.py:271
  25.4 1.2 fusion.2
  26.6 1.3 copy.41.mf_ref
  28.0 27.4 %all-gather.7.cloned.1.call-done = bf16[32,128,128]{2,1,0:T(8,128)(2,1)} async-done(((bf16[2,128,128]{2,1,0:T(8,128)(2,1)}), bf16[32,128,128]{2,1,0:T(8,128)(2,1)}) %all-gather.7.cloned.1.call-update) | async-done | bytes 1048592 | tf_op jit(solution)/shard_map/all_gather | solution.py:268
  55.3 2.4 slice_bitcast_fusion
  57.7 52.7 %all-gather.5.cloned.1.call-done = bf16[8,2,1152,256]{3,2,0,1:T(8,128)(2,1)} async-done(((bf16[1,2,1152,256]{3,2,0,1:T(8,128)(2,1)}), bf16[8,2,1152,256]{3,2,0,1:T(8,128)(2,1)}) %all-gather.5.cloned.1.call-update) | async-done | bytes 9437200 | tf_op jit(solution)/shard_map/all_gather | solution.py:269
  110.4 82.0 %chain.1 = (f32[256,1152]{1,0:T(8,128)}, f32[128,256]{1,0:T(8,128)}) custom-call(bf16[16,128,128]{2,1,0:T(8,128)(2,1)} %get-tuple-element.15.x_ref, bf16[16,128,128]{2,1,0:T(8,128)(2,1)} %get-tuple-element.14.cot_ref, bf16[16,1152,256]{2,1,0:T(8,128)(2,1)} %bitcast.64, bf16[16,256,128]{2,1,0:T(8,128)(2,1)} %copy.41.mf_ref, ...), custom_call_target="tpu_custom_call" | custom-call | tf_op jit(solution)/shard_map/chain/pallas_call | solution.py:202
  192.3 1.6 copy.42
  194.0 0.6 reshape.41
  194.6 0.0 copy-start.1
  194.6 1.2 fusion.4
  195.9 0.0 copy-done.1
  195.9 0.1 pad_maximum_fusion.2
  196.0 1.1 copy.46
  197.2 1.0 reshape_reshape.3
  198.2 1.0 maximum_multiply_fusion
  199.2 0.0 all-reduce.5.cloned.1.call-update
  199.2 0.0 all-reduce.7.cloned.1.call-start
  199.2 61.6 %all-reduce.5.cloned.1.call-done = f32[1792,128]{1,0:T(8,128)} async-done(((f32[1792,128]{1,0:T(8,128)}), f32[1792,128]{1,0:T(8,128)}) %all-reduce.5.cloned.1.call-update) | async-done | bytes 917520 | tf_op jit(solution)/shard_map/psum | solution.py:277
  260.8 1.3 select_bitcast_fusion.1
  262.1 1.4 pad_maximum_fusion
  263.5 0.0 all-reduce.7.cloned.1.call-update
  263.5 91.6 %all-reduce.7.cloned.1.call-done = f32[2,1792,128]{2,1,0:T(8,128)} async-done(((f32[2,1792,128]{2,1,0:T(8,128)}), f32[2,1792,128]{2,1,0:T(8,128)}) %all-reduce.7.cloned.1.call-update) | async-done | bytes 1835024 | tf_op jit(solution)/shard_map/psum | solution.py:281
  355.1 2.8 slice.61
  357.9 1.9 reshape.42
  359.8 1.7 copy.47
  361.4 1.5 slice_bitcast_fusion.5
  (6 shorter events, 0.1 us)
Async XLA Ops:
  7.2 48.2 %all-gather.7.cloned.1.call-start = ((), (), s32[]{:S(2)}) async-start(), calls=%async_computation.3 | async-start | bytes 1114112 | tf_op jit(solution)/shard_map/all_gather | solution.py:268
  8.9 101.5 %all-gather.5.cloned.1.call-start = ((), (), s32[]{:S(2)}) async-start(), calls=%async_computation | async-start | bytes 10616832 | tf_op jit(solution)/shard_map/all_gather | solution.py:269
  10.4 1.2 copy-start
  11.6 249.3 %all-reduce.5.cloned.1.call-start = ((), (), s32[]{:S(2)}) async-start(), calls=%async_computation.1 | async-start | bytes 1835008 | tf_op jit(solution)/shard_map/psum | solution.py:277
  194.6 1.3 copy-start.1
  199.2 155.9 %all-reduce.7.cloned.1.call-start = ((), (), s32[]{:S(2)}) async-start(), calls=%async_computation.2 | async-start | bytes 3670016 | tf_op jit(solution)/shard_map/psum | solution.py:281
Sparse Core Ops, SparseCore 0:
  10.7 44.5 all-gather.6
  57.6 52.7 all-gather.4
  199.3 61.4 all-reduce.4
  264.4 90.6 all-reduce.6

commit v2 on v1

--- a/solution.py
+++ b/solution.py
@@ -1,4 +1,3 @@
-import functools
 import math
 
 import jax
@@ -20,6 +19,12 @@
 TN = (((0,), (0,)), ((), ()))
 FWD_CHUNKS = ((1, 2), (3, 2), (5, 3))
 BWD_CHUNKS = ((1, 2), (3, 2), (5, 3))
+SECTIONS = 8
+SPACES = 16
+TAPS_ROWS = 1728
+GRAD_ROWS = 1792
+PART = GRAD_ROWS // SECTIONS
+FACTOR = 1.0 / math.sqrt(16384.0)
 
 
 def rows_of(start, count):
@@ -41,20 +46,40 @@
 
 
 def chain_kernel(
-    block_shift,
-    x_ref, cot_ref, w_ref, mf_ref, mb_ref,
-    g_ref, gm_ref,
+    tile_ref, w_ref, mf_ref, mb_ref,
+    conv_ref, mix_ref,
     a3a, a3b, act, slope, sa3, shid, pga, pgb,
+    tiles, grad, gsend, gparts, chunk, home,
     fsend, frecv, bsend, brecv,
+    tsend, trecv, psend, precv, hsend, hrecv,
 ):
     section = lax.axis_index("section")
     core = lax.rem(section, 2)
     partner = section + 1 - 2 * core
-    mine = lax.axis_index("space") + block_shift
+    mine = lax.axis_index("space")
     sign = 2 * core - 1
 
     def globally(local):
         return 7 + core + sign * local
+
+    def tile_copy(step, slot):
+        return pltpu.make_async_remote_copy(
+            src_ref=tile_ref,
+            dst_ref=tiles.at[slot],
+            send_sem=tsend.at[step],
+            recv_sem=trecv.at[slot],
+            device_id={"space": lax.rem(mine + step, SPACES)},
+            device_id_type=MESH,
+        )
+
+    needed = jnp.where(core == 0, mine <= 8, mine >= 7)
+
+    @pl.when(needed)
+    def _():
+        for step in range(1, SPACES):
+            tile_copy(step, mine).start()
+
+    tiles[mine] = tile_ref[...]
 
     zeros3 = jnp.zeros((NZ, 3 * KC), BF16)
     for a3 in (a3a, a3b):
@@ -62,7 +87,9 @@
     for pg in (pga, pgb):
         pg[9 * NZ : 10 * NZ, :] = jnp.zeros((NZ, HC), BF16)
     for local in range(-1, PLANES):
-        tile = x_ref[globally(local)].astype(F32)
+        plane = globally(local)
+        pl.when(plane != mine)(lambda plane=plane: tile_copy(1, plane).wait_recv())
+        tile = tiles[plane, 0].astype(F32)
         if local >= 0:
             act[local * NZ : (local + 1) * NZ, :] = tile
         a3a[(local + 1) * NZ : (local + 2) * NZ, :] = widen(tile)
@@ -124,7 +151,7 @@
     lax.fori_loop(0, BLOCKS // 2, forward_pair, 0)
 
     for local in range(PLANES):
-        act[local * NZ : (local + 1) * NZ, :] = cot_ref[globally(local)].astype(F32)
+        act[local * NZ : (local + 1) * NZ, :] = tiles[globally(local), 1].astype(F32)
 
     def backward_prep(pg, block, first, count):
         rows = slice(first * NZ, (first + count) * NZ)
@@ -173,13 +200,22 @@
         def _():
             own = pg[NZ : 9 * NZ, :]
             for dx in range(3):
-                g_ref[:, dx * 384 : (dx + 1) * 384] = lax.dot_general(
-                    own, sa3[rows_of(1 + (dx - 1) * sign, PLANES), :], TN,
+                term = lax.dot_general(
+                    sa3[rows_of(1 + (dx - 1) * sign, PLANES), :], own, TN,
                     preferred_element_type=F32,
                 )
-            gm_ref[...] = lax.dot_general(
+                for dz in range(3):
+                    first = term[dz * KC : dz * KC + 64]
+                    second = term[dz * KC + 64 : (dz + 1) * KC]
+                    folded = (first[:, KC:], first[:, :KC] + second[:, KC:], second[:, :KC])
+                    for dy in range(3):
+                        tap = 9 * dx + 3 * dy + dz
+                        grad[tap * 64 : (tap + 1) * 64, :] = folded[dy]
+            term = lax.dot_general(
                 act[...].astype(BF16), shid[...], TN, preferred_element_type=F32
             )
+            grad[TAPS_ROWS:GRAD_ROWS, :] = term[0:64, :KC] + term[64:128, KC:]
+            gsend[...] = grad[...].astype(BF16)
 
         def rest():
             for first, count in BWD_CHUNKS:
@@ -196,16 +232,85 @@
 
     lax.fori_loop(0, BLOCKS // 2, backward_pair, 0)
 
-
-def run_chain(x, cot, w, mf, mb, block_shift=0):
+    def part_rows(index):
+        return pl.ds(pl.multiple_of(index * PART, PART), PART)
+
+    def part_copy(step):
+        to = lax.rem(section + step, SECTIONS)
+        return pltpu.make_async_remote_copy(
+            src_ref=gsend.at[part_rows(to)],
+            dst_ref=gparts.at[step],
+            send_sem=psend.at[step],
+            recv_sem=precv.at[step],
+            device_id={"section": to},
+            device_id_type=MESH,
+        )
+
+    for step in range(1, SECTIONS):
+        part_copy(step).start()
+
+    @pl.when(needed)
+    def _():
+        for step in range(1, SPACES):
+            tile_copy(step, mine).wait_send()
+
+    total = grad[part_rows(section), :]
+    for step in range(1, SECTIONS):
+        part_copy(step).wait_recv()
+        total = total + gparts[step].astype(F32)
+    chunk[...] = (total * FACTOR).astype(BF16)
+
+    owner = lax.rem(mine, SECTIONS)
+    place = (mine - owner) + section
+
+    def home_copy(step, slot):
+        return pltpu.make_async_remote_copy(
+            src_ref=chunk,
+            dst_ref=home.at[slot],
+            send_sem=hsend.at[step],
+            recv_sem=hrecv.at[slot],
+            device_id={"section": owner, "space": lax.rem(mine + step, SPACES)},
+            device_id_type=MESH,
+        )
+
+    for step in range(1, SPACES):
+        home_copy(step, place).start()
+
+    @pl.when(section != owner)
+    def _():
+        home_copy(0, place).start()
+
+    @pl.when(section == owner)
+    def _():
+        home[place] = chunk[...]
+
+    for step in range(1, SECTIONS):
+        part_copy(step).wait_send()
+
+    for slot in range(2 * SECTIONS):
+        group, part = slot // SECTIONS, slot % SECTIONS
+        here = jnp.logical_and(section == part, mine == group * SECTIONS + section)
+        pl.when(jnp.logical_not(here))(lambda slot=slot: home_copy(1, slot).wait_recv())
+        value = home[slot].astype(F32)
+        rows = min(TAPS_ROWS - part * PART, PART)
+        conv_ref[group, part * PART : part * PART + rows, :] = value[:rows]
+        if rows < PART:
+            mix_ref[group] = value[rows:]
+
+    for step in range(1, SPACES):
+        home_copy(step, place).wait_send()
+    pl.when(section != owner)(lambda: home_copy(0, place).wait_send())
+
+
+def run_chain(tile, w, mf, mb):
     vmem = pl.BlockSpec(memory_space=pltpu.VMEM)
     return pl.pallas_call(
-        functools.partial(chain_kernel, block_shift),
+        chain_kernel,
         out_shape=(
-            jax.ShapeDtypeStruct((HC, 9 * KC), F32),
-            jax.ShapeDtypeStruct((KC, HC), F32),
+            jax.ShapeDtypeStruct((2, TAPS_ROWS, 128), F32),
+            jax.ShapeDtypeStruct((2, 64, 128), F32),
         ),
-        in_specs=[vmem] * 5,
+        in_specs=[vmem] * 4,
         out_specs=(vmem, vmem),
         scratch_shapes=[
             pltpu.VMEM((10 * NZ, 3 * KC), BF16),
@@ -216,16 +321,28 @@
             pltpu.VMEM((PLANES * NZ, HC), BF16),
             pltpu.VMEM((10 * NZ, HC), BF16),
             pltpu.VMEM((10 * NZ, HC), BF16),
+            pltpu.VMEM((SPACES, 2, NZ, KC), BF16),
+            pltpu.VMEM((GRAD_ROWS, 128), F32),
+            pltpu.VMEM((GRAD_ROWS, 128), BF16),
+            pltpu.VMEM((SECTIONS, PART, 128), BF16),
+            pltpu.VMEM((PART, 128), BF16),
+            pltpu.VMEM((2 * SECTIONS, PART, 128), BF16),
             pltpu.SemaphoreType.DMA((2,)),
             pltpu.SemaphoreType.DMA((2,)),
             pltpu.SemaphoreType.DMA((2,)),
             pltpu.SemaphoreType.DMA((2,)),
+            pltpu.SemaphoreType.DMA((SPACES,)),
+            pltpu.SemaphoreType.DMA((SPACES,)),
+            pltpu.SemaphoreType.DMA((SECTIONS,)),
+            pltpu.SemaphoreType.DMA((SECTIONS,)),
+            pltpu.SemaphoreType.DMA((SPACES,)),
+            pltpu.SemaphoreType.DMA((2 * SECTIONS,)),
         ],
         compiler_params=pltpu.CompilerParams(
             has_side_effects=True, vmem_limit_bytes=60 * 1024 * 1024
         ),
         name="chain",
-    )(x, cot, w, mf, mb)
+    )(tile, w, mf, mb)
 
 
 def conv_matrix(conv_w):
@@ -243,46 +360,21 @@
     )
 
 
-def fold_conv(grad):
-    parts = grad.reshape(2, 128, 3, 3, 2, 64)
-    mid = parts[0, :, :, :, 0] + parts[1, :, :, :, 1]
-    low = parts[1, :, :, :, 0]
-    high = parts[0, :, :, :, 1]
-    return jnp.stack([low, mid, high], axis=2).reshape(128, 1728)
-
-
-def fold_mix(grad):
-    return grad[0:64, 0:128] + grad[64:128, 128:256]
-
-
 def plane_rows(tile):
     return tile[:, 0].transpose(2, 1, 0).reshape(NZ, KC)
 
 
 def per_device(inputs, cotangent, conv_weight, mix_weight):
-    section = lax.axis_index("section")
-    space = lax.axis_index("space")
-    micro = section // 2
+    micro = lax.axis_index("section") // 2
     x = plane_rows(lax.dynamic_index_in_dim(inputs, micro, 0, keepdims=False))
     cot = plane_rows(lax.dynamic_index_in_dim(cotangent, micro, 0, keepdims=False))
-    both = lax.all_gather(jnp.stack([x, cot], 0), "space")
     w = lax.all_gather(conv_matrix(conv_weight[:, 0]), "section")
     w = w.transpose(1, 0, 2, 3).reshape(BLOCKS, 9 * KC, HC)
     mix = lax.all_gather(mix_weight[:, 0], "section").transpose(1, 0, 2, 3).reshape(BLOCKS, 64, 128)
     mb = mix_matrix(mix)
     mf = mb.transpose(0, 2, 1)
-    grad, grad_mix = run_chain(both[:, 0], both[:, 1], w, mf, mb)
-    factor = 1.0 / math.sqrt(16384.0)
-    part = jnp.concatenate([fold_conv(grad).reshape(-1, 128), fold_mix(grad_mix)], 0) * factor
-    part = lax.psum(part, "section")
-    slot = jnp.stack(
-        [jnp.where(space == section, part, 0.0), jnp.where(space == section + 8, part, 0.0)], 0
-    )
-    total = lax.psum(slot, "space")
-    return (
-        total[:, :1728].reshape(2, 1, 128, 1728),
-        total[:, 1728:].reshape(2, 1, 64, 128),
-    )
+    conv_grad, mix_grad = run_chain(jnp.stack([x, cot], 0), w, mf, mb)
+    return conv_grad.transpose(0, 2, 1)[:, None], mix_grad[:, None]
 
 
 def solution(mesh):

time: 370 us -> 204 us (0.55)
  the two profiles are of different devices: /device:TPU:32 before, /device:TPU:104 now
where the time goes in v2:
time: 204 us
  Pallas kernels  130 us (64%)
  waiting for transfers between devices  36.7 us (18%)
  between operations  14.1 us (7%)
  blocking collectives  12.8 us (6%)
  local copies, waits for them, and re-layouts  8.25 us (4%)
  other arithmetic  2.09 us (1%)
    pallas_call x1, Pallas kernels, run_chain(): pl.pallas_call(chain_kernel, out_shape=(jax.ShapeDtypeStruct((2, TAPS_ROW...  130 us
    all_gather x1, waiting for transfers between devices, per_device(): w = lax.all_gather(conv_matrix(conv_weight[:, 0]), 'section')  36.7 us
    all_gather x1, blocking collectives, per_device(): lax.all_gather(mix_weight[:, 0], 'section').transpose(1, 0, 2, 3)  12.8 us
  transfers between devices with their start and end apart: 1, of which 1 were waited for; matrix products, arithmetic and copies ran while one was open for 2% of the time, Pallas kernels for 0%

profile of v2, /device:TPU:104, one launch (start us, length us, event | category | flops | bytes accessed | tf_op | source)
XLA Modules:
  0.0 203.8 jit_solution(1036604617842476633)
XLA Ops:
  7.2 0.0 all-gather.3.cloned.1.call-start
  7.2 1.2 slice_bitcast_fusion.1
  8.4 0.1 maximum_bitcast_fusion
  8.6 0.1 pad_maximum_fusion
  8.7 1.1 copy.30
  9.8 0.0 copy-start.1
  9.8 0.0 all-gather.3.cloned.1.call-update
  9.9 0.8 constant_dynamic-slice_fusion
  10.7 0.1 copy.27
  10.8 0.1 copy.26
  11.0 0.0 copy-done.1
  11.0 12.8 %all-gather = bf16[16,1,64,128]{3,2,1,0:T(8,128)(2,1)S(1)} all-gather(bf16[2,1,64,128]{3,2,1,0:T(8,128)(2,1)S(1)} %copy-done.1), channel_id=2, replica_groups=mesh['section'=8,'space'=16] {'section'}, dimensions={0}, use_global_device_ids=true | all-gather | bytes 294912 | tf_op jit(solution)/shard_map/all_gather | solution.py:373
  23.8 1.2 fusion.2
  25.0 1.4 copy.32.mf_ref
  26.4 0.6 pad_maximum_fusion.1.tile_ref
  27.0 36.7 %all-gather.3.cloned.1.call-done = bf16[8,2,1152,256]{3,2,0,1:T(8,128)(2,1)} async-done(((bf16[1,2,1152,256]{3,2,0,1:T(8,128)(2,1)}), bf16[8,2,1152,256]{3,2,0,1:T(8,128)(2,1)}) %all-gather.3.cloned.1.call-update) | async-done | bytes 9437200 | tf_op jit(solution)/shard_map/all_gather | solution.py:371
  63.7 129.8 %chain.1 = (f32[2,1728,128]{2,1,0:T(8,128)}, f32[2,64,128]{2,1,0:T(8,128)}) custom-call(bf16[2,128,128]{2,1,0:T(8,128)(2,1)} %pad_maximum_fusion.1.tile_ref, bf16[16,1152,256]{2,1,0:T(8,128)(2,1)} %bitcast.45, bf16[16,256,128]{2,1,0:T(8,128)(2,1)} %copy.32.mf_ref, bf16[16,128,256]{2,1,0:T(8,128)(2,1)} %get-tuple-element.17.mb_ref), custom_call_target="tpu_custom_call" | custom-call | tf_op jit(solution)/shard_map/chain/pallas_call | solution.py:307
  193.5 0.0 copy-start
  193.5 2.8 %copy.41 = f32[2,1,128,1728]{2,3,1,0:T(8,128)} copy(f32[2,1,128,1728]{2,3,1,0:T(8,128)} %bitcast.47) | data formatting | bytes 3538944
  196.3 0.0 copy-done
  196.3 0.6 copy.42
  (3 shorter events, 0.0 us)
Async XLA Ops:
  7.2 56.5 %all-gather.3.cloned.1.call-start = ((), (), s32[]{:S(2)}) async-start(), calls=%async_computation | async-start | bytes 10616832 | tf_op jit(solution)/shard_map/all_gather | solution.py:371
  9.8 1.1 copy-start.1
  193.5 2.8 %copy-start = (f32[2,64,128]{2,1,0:T(8,128)S(1)}, f32[2,64,128]{2,1,0:T(8,128)}, u32[]{:S(2)}) copy-start(f32[2,64,128]{2,1,0:T(8,128)} %get-tuple-element.5) | copy-start | bytes 196612
Sparse Core Ops, SparseCore 0:
  10.3 53.3 all-gather.2

commit v3 on v2

--- a/solution.py
+++ b/solution.py
@@ -46,12 +46,14 @@
 
 
 def chain_kernel(
-    tile_ref, w_ref, mf_ref, mb_ref,
+    tile_ref, wt_ref, mt_ref,
     conv_ref, mix_ref,
     a3a, a3b, act, slope, sa3, shid, pga, pgb,
     tiles, grad, gsend, gparts, chunk, home,
+    wraw, mraw, w_ref, mb_ref,
     fsend, frecv, bsend, brecv,
     tsend, trecv, psend, precv, hsend, hrecv,
+    wsend, msend, wrelay, mrelay, wrecv, mrecv,
 ):
     section = lax.axis_index("section")
     core = lax.rem(section, 2)
@@ -79,7 +81,80 @@
         for step in range(1, SPACES):
             tile_copy(step, mine).start()
 
+    def weight_copies(group, hop):
+        to = partner if hop == 0 else lax.rem(section + 2 * hop, SECTIONS)
+        block = group * SECTIONS + section
+        return [
+            pltpu.make_async_remote_copy(
+                src_ref=src.at[group],
+                dst_ref=dst.at[block],
+                send_sem=send.at[group, hop],
+                recv_sem=recv.at[block],
+                device_id={"section": to},
+                device_id_type=MESH,
+            )
+            for src, dst, send, recv in (
+                (wt_ref, wraw, wsend, wrecv), (mt_ref, mraw, msend, mrecv)
+            )
+        ]
+
+    def relay_copies(block):
+        return [
+            pltpu.make_async_remote_copy(
+                src_ref=buf.at[block],
+                dst_ref=buf.at[block],
+                send_sem=send.at[block],
+                recv_sem=recv.at[block],
+                device_id={"section": partner},
+                device_id_type=MESH,
+            )
+            for buf, send, recv in ((wraw, wrelay, wrecv), (mraw, mrelay, mrecv))
+        ]
+
+    for group in range(2):
+        for hop in (0, 1, 3, 2):
+            for copy in weight_copies(group, hop):
+                copy.start()
+        wraw[group * SECTIONS + section] = wt_ref[group]
+        mraw[group * SECTIONS + section] = mt_ref[group]
+
+    def relayed_here(block):
+        return jnp.logical_and(lax.rem(block, 2) == core, lax.rem(block, SECTIONS) != section)
+
+    def pass_on(block):
+        @pl.when(relayed_here(block))
+        def _():
+            for copy in relay_copies(block):
+                copy.wait_recv()
+            for copy in relay_copies(block):
+                copy.start()
+
+    def expand(block):
+        @pl.when(lax.rem(block, 2) != core)
+        def _():
+            for copy in relay_copies(block):
+                copy.wait_recv()
+
+        for dx in range(3):
+            for dz in range(3):
+                row = (3 * dx + dz) * KC
+                low, mid, high = (
+                    wraw[block, (9 * dx + 3 * dy + dz) * 64 : (9 * dx + 3 * dy + dz + 1) * 64, :]
+                    for dy in range(3)
+                )
+                w_ref[block, row : row + 64, 0:128] = mid
+                w_ref[block, row : row + 64, 128:256] = low
+                w_ref[block, row + 64 : row + 128, 0:128] = high
+                w_ref[block, row + 64 : row + 128, 128:256] = mid
+        empty = jnp.zeros((64, 128), BF16)
+        mb_ref[block, 0:64, 0:128] = mraw[block]
+        mb_ref[block, 0:64, 128:256] = empty
+        mb_ref[block, 64:128, 0:128] = empty
+        mb_ref[block, 64:128, 128:256] = mraw[block]
+
     tiles[mine] = tile_ref[...]
+    pass_on(0)
+    pass_on(1)
 
     zeros3 = jnp.zeros((NZ, 3 * KC), BF16)
     for a3 in (a3a, a3b):
@@ -114,7 +189,9 @@
         def _():
             shid[rows, :] = hid
 
-        new = act[rows, :] + jnp.dot(hid, mf_ref[block], preferred_element_type=F32)
+        new = act[rows, :] + lax.dot_general(
+            hid, mb_ref[block], NT, preferred_element_type=F32
+        )
         act[rows, :] = new
         nxt[(first + 1) * NZ : (first + 1 + count) * NZ, :] = widen(new)
 
@@ -129,6 +206,7 @@
         )
 
     def forward_block(block, cur, nxt, par, wait, send):
+        expand(block)
         for first, count in FWD_CHUNKS:
             forward_planes(cur, nxt, block, first, count)
         wait(lambda: act_copy(cur, par).wait())
@@ -139,6 +217,7 @@
 
         forward_planes(cur, nxt, block, 0, 1)
         send(lambda: act_copy(nxt, 1 - par).start())
+        pl.when(block < BLOCKS - 2)(lambda: pass_on(block + 2))
 
     def always(go):
         go()
@@ -149,6 +228,16 @@
         return carry
 
     lax.fori_loop(0, BLOCKS // 2, forward_pair, 0)
+
+    for group in range(2):
+        for hop in range(4):
+            for copy in weight_copies(group, hop):
+                copy.wait_send()
+    for block in range(BLOCKS):
+        @pl.when(relayed_here(block))
+        def _(block=block):
+            for copy in relay_copies(block):
+                copy.wait_send()
 
     for local in range(PLANES):
         act[local * NZ : (local + 1) * NZ, :] = tiles[globally(local), 1].astype(F32)
@@ -302,7 +391,7 @@
     pl.when(section != owner)(lambda: home_copy(0, place).wait_send())
 
 
-def run_chain(tile, w, mf, mb):
+def run_chain(tile, w, mix):
     vmem = pl.BlockSpec(memory_space=pltpu.VMEM)
     return pl.pallas_call(
         chain_kernel,
@@ -310,7 +399,7 @@
             jax.ShapeDtypeStruct((2, TAPS_ROWS, 128), F32),
             jax.ShapeDtypeStruct((2, 64, 128), F32),
         ),
-        in_specs=[vmem] * 4,
+        in_specs=[vmem] * 3,
         out_specs=(vmem, vmem),
         scratch_shapes=[
             pltpu.VMEM((10 * NZ, 3 * KC), BF16),
@@ -327,6 +416,10 @@
             pltpu.VMEM((SECTIONS, PART, 128), BF16),
             pltpu.VMEM((PART, 128), BF16),
             pltpu.VMEM((2 * SECTIONS, PART, 128), BF16),
+            pltpu.VMEM((BLOCKS, TAPS_ROWS, 128), BF16),
+            pltpu.VMEM((BLOCKS, 64, 128), BF16),
+            pltpu.VMEM((BLOCKS, 9 * KC, HC), BF16),
+            pltpu.VMEM((BLOCKS, KC, HC), BF16),
             pltpu.SemaphoreType.DMA((2,)),
             pltpu.SemaphoreType.DMA((2,)),
             pltpu.SemaphoreType.DMA((2,)),
@@ -337,27 +430,18 @@
             pltpu.SemaphoreType.DMA((SECTIONS,)),
             pltpu.SemaphoreType.DMA((SPACES,)),
             pltpu.SemaphoreType.DMA((2 * SECTIONS,)),
+            pltpu.SemaphoreType.DMA((2, 4)),
+            pltpu.SemaphoreType.DMA((2, 4)),
+            pltpu.SemaphoreType.DMA((BLOCKS,)),
+            pltpu.SemaphoreType.DMA((BLOCKS,)),
+            pltpu.SemaphoreType.DMA((BLOCKS,)),
+            pltpu.SemaphoreType.DMA((BLOCKS,)),
         ],
         compiler_params=pltpu.CompilerParams(
             has_side_effects=True, vmem_limit_bytes=60 * 1024 * 1024
         ),
         name="chain",
-    )(tile, w, mf, mb)
-
-
-def conv_matrix(conv_w):
-    taps = conv_w.reshape(-1, 128, 3, 3, 3, 64).transpose(0, 2, 3, 4, 5, 1)
-    low, mid, high = taps[:, :, 0], taps[:, :, 1], taps[:, :, 2]
-    top = jnp.concatenate([mid, low], axis=-1)
-    bottom = jnp.concatenate([high, mid], axis=-1)
-    return jnp.stack([top, bottom], axis=3).reshape(-1, 9 * KC, HC)
-
-
-def mix_matrix(mix_w):
-    empty = jnp.zeros_like(mix_w)
-    return jnp.concatenate(
-        [jnp.concatenate([mix_w, empty], 2), jnp.concatenate([empty, mix_w], 2)], 1
-    )
+    )(tile, w, mix)
 
 
 def plane_rows(tile):
@@ -368,12 +452,8 @@
     micro = lax.axis_index("section") // 2
     x = plane_rows(lax.dynamic_index_in_dim(inputs, micro, 0, keepdims=False))
     cot = plane_rows(lax.dynamic_index_in_dim(cotangent, micro, 0, keepdims=False))
-    w = lax.all_gather(conv_matrix(conv_weight[:, 0]), "section")
-    w = w.transpose(1, 0, 2, 3).reshape(BLOCKS, 9 * KC, HC)
-    mix = lax.all_gather(mix_weight[:, 0], "section").transpose(1, 0, 2, 3).reshape(BLOCKS, 64, 128)
-    mb = mix_matrix(mix)
-    mf = mb.transpose(0, 2, 1)
-    conv_grad, mix_grad = run_chain(jnp.stack([x, cot], 0), w, mf, mb)
+    w = conv_weight[:, 0].transpose(0, 2, 1)
+    conv_grad, mix_grad = run_chain(jnp.stack([x, cot], 0), w, mix_weight[:, 0])
     return conv_grad.transpose(0, 2, 1)[:, None], mix_grad[:, None]
 
 

time: 204 us -> 144 us (0.71)
  the two profiles are of different devices: /device:TPU:104 before, /device:TPU:32 now
where the time goes in v3:
time: 144 us; the launch traced here: 143 us
  Pallas kernels  137 us (95%)
  local copies, waits for them, and re-layouts  4.53 us (3%)
    pallas_call x1, Pallas kernels, run_chain(): pl.pallas_call(chain_kernel, out_shape=(jax.ShapeDtypeStruct((2, TAPS_ROW...  137 us
    unnamed x6, local copies, waits for them, and re-layouts  3.48 us

profile of v3, /device:TPU:32, one launch (start us, length us, event | category | flops | bytes accessed | tf_op | source)
XLA Modules:
  0.0 143.3 jit_solution(13743476948973225312)
XLA Ops:
  0.6 0.8 constant_dynamic-slice_fusion
  1.5 0.1 copy.11
  1.6 0.1 copy.10
  1.7 0.6 pad_maximum_fusion.tile_ref
  2.4 137.4 %chain.1 = (f32[2,1728,128]{2,1,0:T(8,128)}, f32[2,64,128]{2,1,0:T(8,128)}) custom-call(bf16[2,128,128]{2,1,0:T(8,128)(2,1)} %pad_maximum_fusion.tile_ref, bf16[2,1728,128]{2,1,0:T(8,128)(2,1)} %bitcast.23, bf16[2,64,128]{2,1,0:T(8,128)(2,1)} %bitcast.27), custom_call_target="tpu_custom_call" | custom-call | tf_op jit(solution)/shard_map/chain/pallas_call | solution.py:396
  139.8 0.0 copy-start
  139.8 2.8 %copy.18 = f32[2,1,128,1728]{2,3,1,0:T(8,128)} copy(f32[2,1,128,1728]{2,3,1,0:T(8,128)} %bitcast.22) | data formatting | bytes 3538944
  142.7 0.0 copy-done
  142.7 0.6 copy.19
  (2 shorter events, 0.0 us)
Async XLA Ops:
  139.8 2.8 %copy-start = (f32[2,64,128]{2,1,0:T(8,128)S(1)}, f32[2,64,128]{2,1,0:T(8,128)}, u32[]{:S(2)}) copy-start(f32[2,64,128]{2,1,0:T(8,128)} %get-tuple-element.5) | copy-start | bytes 196612

commit v4 on v3

--- a/solution.py
+++ b/solution.py
@@ -279,6 +279,50 @@
             device_id_type=MESH,
         )
 
+    def part_rows(index):
+        return pl.ds(pl.multiple_of(index * PART, PART), PART)
+
+    def part_copy(step):
+        to = lax.rem(section + step, SECTIONS)
+        return pltpu.make_async_remote_copy(
+            src_ref=gsend.at[part_rows(to)],
+            dst_ref=gparts.at[step],
+            send_sem=psend.at[step],
+            recv_sem=precv.at[step],
+            device_id={"section": to},
+            device_id_type=MESH,
+        )
+
+    owner = lax.rem(mine, SECTIONS)
+    place = (mine - owner) + section
+
+    def home_copy(step, slot):
+        return pltpu.make_async_remote_copy(
+            src_ref=chunk,
+            dst_ref=home.at[slot],
+            send_sem=hsend.at[step],
+            recv_sem=hrecv.at[slot],
+            device_id={"section": owner, "space": lax.rem(mine + step, SPACES)},
+            device_id_type=MESH,
+        )
+
+    def finish_parts():
+        total = grad[part_rows(section), :]
+        for step in range(1, SECTIONS):
+            part_copy(step).wait_recv()
+            total = total + gparts[step].astype(F32)
+        chunk[...] = (total * FACTOR).astype(BF16)
+        for step in range(1, SPACES):
+            home_copy(step, place).start()
+
+        @pl.when(section != owner)
+        def _():
+            home_copy(0, place).start()
+
+        @pl.when(section == owner)
+        def _():
+            home[place] = chunk[...]
+
     def backward_block(block, pg, par, last):
         backward_prep(pg, block, 0, 1)
         last(lambda: grad_copy(pg, par).start())
@@ -305,6 +349,8 @@
             )
             grad[TAPS_ROWS:GRAD_ROWS, :] = term[0:64, :KC] + term[64:128, KC:]
             gsend[...] = grad[...].astype(BF16)
+            for step in range(1, SECTIONS):
+                part_copy(step).start()
 
         def rest():
             for first, count in BWD_CHUNKS:
@@ -313,6 +359,7 @@
             backward_planes(pg, block, 0, 1)
 
         last(rest)
+        pl.when(block == mine - 2)(finish_parts)
 
     def backward_pair(step, carry):
         backward_block(15 - 2 * step, pga, 0, always)
@@ -321,57 +368,12 @@
 
     lax.fori_loop(0, BLOCKS // 2, backward_pair, 0)
 
-    def part_rows(index):
-        return pl.ds(pl.multiple_of(index * PART, PART), PART)
-
-    def part_copy(step):
-        to = lax.rem(section + step, SECTIONS)
-        return pltpu.make_async_remote_copy(
-            src_ref=gsend.at[part_rows(to)],
-            dst_ref=gparts.at[step],
-            send_sem=psend.at[step],
-            recv_sem=precv.at[step],
-            device_id={"section": to},
-            device_id_type=MESH,
-        )
-
-    for step in range(1, SECTIONS):
-        part_copy(step).start()
-
     @pl.when(needed)
     def _():
         for step in range(1, SPACES):
             tile_copy(step, mine).wait_send()
 
-    total = grad[part_rows(section), :]
-    for step in range(1, SECTIONS):
-        part_copy(step).wait_recv()
-        total = total + gparts[step].astype(F32)
-    chunk[...] = (total * FACTOR).astype(BF16)
-
-    owner = lax.rem(mine, SECTIONS)
-    place = (mine - owner) + section
-
-    def home_copy(step, slot):
-        return pltpu.make_async_remote_copy(
-            src_ref=chunk,
-            dst_ref=home.at[slot],
-            send_sem=hsend.at[step],
-            recv_sem=hrecv.at[slot],
-            device_id={"section": owner, "space": lax.rem(mine + step, SPACES)},
-            device_id_type=MESH,
-        )
-
-    for step in range(1, SPACES):
-        home_copy(step, place).start()
-
-    @pl.when(section != owner)
-    def _():
-        home_copy(0, place).start()
-
-    @pl.when(section == owner)
-    def _():
-        home[place] = chunk[...]
+    pl.when(mine < 2)(finish_parts)
 
     for step in range(1, SECTIONS):
         part_copy(step).wait_send()

time: 144 us -> 138 us (0.958)
  Pallas kernels: 137 us -> 132 us
    pallas_call x1, Pallas kernels: 137 us -> 132 us  [run_chain(): pl.pallas_call(chain_kernel, out_shape=(jax.ShapeDtypeStruct((2, TAPS_ROW...]
where the time goes in v4:
time: 138 us; the launch traced here: 137 us
  Pallas kernels  132 us (96%)
  local copies, waits for them, and re-layouts  4.53 us (3%)
    pallas_call x1, Pallas kernels, run_chain(): pl.pallas_call(chain_kernel, out_shape=(jax.ShapeDtypeStruct((2, TAPS_ROW...  132 us
    unnamed x6, local copies, waits for them, and re-layouts  3.48 us

profile of v4, /device:TPU:32, one launch (start us, length us, event | category | flops | bytes accessed | tf_op | source)
XLA Modules:
  0.0 137.4 jit_solution(12672115347847130962)
XLA Ops:
  0.6 0.8 constant_dynamic-slice_fusion
  1.5 0.1 copy.11
  1.6 0.1 copy.10
  1.7 0.6 pad_maximum_fusion.tile_ref
  2.4 131.5 %chain.1 = (f32[2,1728,128]{2,1,0:T(8,128)}, f32[2,64,128]{2,1,0:T(8,128)}) custom-call(bf16[2,128,128]{2,1,0:T(8,128)(2,1)} %pad_maximum_fusion.tile_ref, bf16[2,1728,128]{2,1,0:T(8,128)(2,1)} %bitcast.23, bf16[2,64,128]{2,1,0:T(8,128)(2,1)} %bitcast.27), custom_call_target="tpu_custom_call" | custom-call | tf_op jit(solution)/shard_map/chain/pallas_call | solution.py:398
  133.9 0.0 copy-start
  133.9 2.8 %copy.18 = f32[2,1,128,1728]{2,3,1,0:T(8,128)} copy(f32[2,1,128,1728]{2,3,1,0:T(8,128)} %bitcast.22) | data formatting | bytes 3538944
  136.8 0.0 copy-done
  136.8 0.6 copy.19
  (2 shorter events, 0.0 us)
Async XLA Ops:
  133.9 2.8 %copy-start = (f32[2,64,128]{2,1,0:T(8,128)S(1)}, f32[2,64,128]{2,1,0:T(8,128)}, u32[]{:S(2)}) copy-start(f32[2,64,128]{2,1,0:T(8,128)} %get-tuple-element.5) | copy-start | bytes 196612

commit v5 on v4

--- a/solution.py
+++ b/solution.py
@@ -382,7 +382,7 @@
         group, part = slot // SECTIONS, slot % SECTIONS
         here = jnp.logical_and(section == part, mine == group * SECTIONS + section)
         pl.when(jnp.logical_not(here))(lambda slot=slot: home_copy(1, slot).wait_recv())
-        value = home[slot].astype(F32)
+        value = home[slot]
         rows = min(TAPS_ROWS - part * PART, PART)
         conv_ref[group, part * PART : part * PART + rows, :] = value[:rows]
         if rows < PART:
@@ -398,8 +398,8 @@
     return pl.pallas_call(
         chain_kernel,
         out_shape=(
-            jax.ShapeDtypeStruct((2, TAPS_ROWS, 128), F32),
-            jax.ShapeDtypeStruct((2, 64, 128), F32),
+            jax.ShapeDtypeStruct((2, TAPS_ROWS, 128), BF16),
+            jax.ShapeDtypeStruct((2, 64, 128), BF16),
         ),
         in_specs=[vmem] * 3,
         out_specs=(vmem, vmem),
@@ -456,7 +456,10 @@
     cot = plane_rows(lax.dynamic_index_in_dim(cotangent, micro, 0, keepdims=False))
     w = conv_weight[:, 0].transpose(0, 2, 1)
     conv_grad, mix_grad = run_chain(jnp.stack([x, cot], 0), w, mix_weight[:, 0])
-    return conv_grad.transpose(0, 2, 1)[:, None], mix_grad[:, None]
+    return (
+        conv_grad.astype(F32).transpose(0, 2, 1)[:, None],
+        mix_grad.astype(F32)[:, None],
+    )
 
 
 def solution(mesh):

time: 138 us -> 137 us (level)
  local copies, waits for them, and re-layouts: 4.53 us -> 1.07 us
  other arithmetic: 0.65 us -> 3.78 us
    unnamed x6 -> x4, local copies, waits for them, and re-layouts: 3.48 us -> 0.02 us
    unnamed x0 -> x2, other arithmetic: none -> 3.13 us
where the time goes in v5:
time: 137 us
  Pallas kernels  131 us (96%)
  other arithmetic  3.78 us (3%)
    pallas_call x1, Pallas kernels, run_chain(): pl.pallas_call(chain_kernel, out_shape=(jax.ShapeDtypeStruct((2, TAPS_ROW...  131 us
    unnamed x2, other arithmetic  3.13 us

profile of v5, /device:TPU:32, one launch (start us, length us, event | category | flops | bytes accessed | tf_op | source)
XLA Modules:
  0.0 136.7 jit_solution(6162962802248675931)
XLA Ops:
  0.6 0.8 constant_dynamic-slice_fusion
  1.5 0.1 copy.10
  1.6 0.1 copy.11
  1.7 0.6 pad_maximum_fusion.tile_ref
  2.4 131.1 %chain.1 = (bf16[2,1728,128]{2,1,0:T(8,128)(2,1)}, bf16[2,64,128]{2,1,0:T(8,128)(2,1)}) custom-call(bf16[2,128,128]{2,1,0:T(8,128)(2,1)} %pad_maximum_fusion.tile_ref, bf16[2,1728,128]{2,1,0:T(8,128)(2,1)} %bitcast.26, bf16[2,64,128]{2,1,0:T(8,128)(2,1)} %bitcast.29), custom_call_target="tpu_custom_call" | custom-call | tf_op jit(solution)/shard_map/chain/pallas_call | solution.py:398
  133.5 0.0 copy-start
  133.5 2.5 %convert_bitcast_fusion = f32[2,1,128,1728]{2,3,1,0:T(8,128)} fusion(bf16[2,1728,128]{2,1,0:T(8,128)(2,1)} %get-tuple-element.4), kind=kLoop, calls=%fused_computation | loop fusion | flops 442368 | bytes 2654208
  136.0 0.0 copy-done
  136.0 0.6 bitcast_convert_fusion
  (2 shorter events, 0.0 us)
Async XLA Ops:
  133.5 2.5 %copy-start = (bf16[2,64,128]{2,1,0:T(8,128)(2,1)S(1)}, bf16[2,64,128]{2,1,0:T(8,128)(2,1)}, u32[]{:S(2)}) copy-start(bf16[2,64,128]{2,1,0:T(8,128)(2,1)} %get-tuple-element.5) | copy-start | bytes 98308
